TPU v7x, 32 devices: a whole 2x2x4 slice. The times are simulated.
32 devices in a mesh: groups: 2 (over y), chan: 4 (over z), tm: 2 (over x), sub: 2 (over core).
Axes of the slice: x: 2, y: 2, z: 4, core: 2. Of those that a mesh axis runs over, the one named last changes fastest.
Arguments:
- traces: float32 [2048, 8192], P(('groups', 'chan', 'sub'), 'tm'), parts along dimension 0, may hold values from -6 to 6
- filters: float32 [2048, 65], P(('groups', 'chan', 'sub')), parts along dimension 0, may hold values from -0.75 to 0.75
- sources: int32 [256], P('groups'), parts along dimension 0, may hold values from 0 to 1023, as said below
Outputs:
- corr: float32 [128, 129, 2048], P('tm', None, ('groups', 'chan', 'sub')), parts along dimension 2
There are 2 independent parts, one for each index of `groups`. A program takes and returns all parts, laid end to end along the dimension named above; each array names one. Nothing has to cross between parts.
Inputs may be any that keep to these rules, and one draw needn't show every extreme that they name: `sources`: the 128 partner channels are distinct. No block of 128 consecutive channels starting at a multiple of 128 holds more than 16 of them, and some block holds exactly 16.
All inputs are finite; a program needn't handle non-finite values.
Results may differ from a plain program's by a relative error of at most 0.0033.
Values may be sent and summed in bfloat16 or wider, within the bound.
A program may use at most 64 MiB of HBM per device.

v0:
```python
import math
import jax
import jax.numpy as jnp
from jax import lax
from jax.sharding import PartitionSpec as P

LAGS = 129


def padded_2(block, sides, width):
    for axis, dim in sides:
        count = lax.axis_size(axis)
        forward = [(i, i + 1) for i in range(count - 1)]
        backward = [(target, source) for source, target in forward]
        low = lax.ppermute(
            lax.slice_in_dim(block, block.shape[dim] - width, None, axis=dim), axis, forward
        )
        high = lax.ppermute(lax.slice_in_dim(block, 0, width, axis=dim), axis, backward)
        block = jnp.concatenate([low, block, high], axis=dim)
    return block


def whiten(extended, filters, out_len):
    running = jnp.zeros((extended.shape[0], out_len), jnp.float32)
    for k in range(filters.shape[1]):
        running = running + filters[:, k : k + 1] * extended[:, k : k + out_len]
    return running


def correlate(padded_seg, part_rows):
    seg_len = part_rows.shape[1]
    block_len = min(512, seg_len)
    block_count = seg_len // block_len

    def advance(block_index, summed):
        offset = block_index * block_len
        window = lax.dynamic_slice_in_dim(padded_seg, offset, block_len + LAGS - 1, 1)
        rows_here = lax.dynamic_slice_in_dim(part_rows, offset, block_len, 1)
        term = lax.conv_general_dilated(
            window[:, None, :],
            rows_here[:, None, :],
            (1,),
            "VALID",
            dimension_numbers=("NCH", "OIH", "NCH"),
            preferred_element_type=jnp.float32,
        )
        return summed + term

    start_sum = jnp.zeros((padded_seg.shape[0], part_rows.shape[0], LAGS), jnp.float32)
    return lax.fori_loop(0, block_count, advance, start_sum)


def on_device(traces, filters, sources):
    chan_dev, seg_len = traces.shape
    taps = filters.shape[1]
    half_taps = (taps - 1) // 2
    half_lags = (LAGS - 1) // 2
    partner_count = sources.shape[0]
    time_devs = lax.axis_size("tm")
    extended = padded_2(traces, (("tm", 1),), half_taps + half_lags)
    whitened_ext = whiten(extended, filters, seg_len + 2 * half_lags)
    position = (
        lax.axis_index("tm") * seg_len
        - half_lags
        + jnp.arange(seg_len + 2 * half_lags, dtype=jnp.int32)
    )
    inside = (position >= 0) & (position < seg_len * time_devs)
    padded = jnp.where(inside[None, :], whitened_ext, 0.0).astype(jnp.bfloat16)
    whitened = padded[:, half_lags : half_lags + seg_len]
    my_block = lax.axis_index(("chan", "sub"))
    owners = sources // chan_dev
    within = sources % chan_dev
    is_mine = owners == my_block
    chan_ids = jnp.arange(chan_dev, dtype=jnp.int32)
    slot_most = min(chan_dev, partner_count // 8)
    order_ids = jnp.arange(partner_count, dtype=jnp.int32)
    same_owner = owners[:, None] == owners[None, :]
    earlier = order_ids[None, :] < order_ids[:, None]
    rank_in = jnp.sum((same_owner & earlier).astype(jnp.int32), axis=1)
    choose = (
        (rank_in[None, :] == jnp.arange(slot_most, dtype=jnp.int32)[:, None]) & is_mine[None, :]
    ).astype(jnp.bfloat16)
    onehot = (within[:, None] == chan_ids[None, :]).astype(jnp.bfloat16)
    picker = jnp.dot(choose, onehot, preferred_element_type=jnp.float32).astype(jnp.bfloat16)
    slot_rows = jnp.dot(picker, whitened, preferred_element_type=jnp.float32).astype(jnp.bfloat16)
    slot_id = owners * slot_most + rank_in
    segment = lax.all_gather(slot_rows, ("chan", "sub"), axis=0, tiled=True)
    row_count = segment.shape[0]
    select = (slot_id[:, None] == jnp.arange(row_count, dtype=jnp.int32)[None, :]).astype(
        jnp.bfloat16
    )
    partners = jnp.dot(select, segment, preferred_element_type=jnp.float32).astype(jnp.bfloat16)
    norm_scale = 1.0 / math.sqrt(seg_len * time_devs)
    summed = correlate(padded, partners)
    return lax.psum_scatter(
        jnp.transpose(summed[:, :, ::-1], (1, 2, 0)) * norm_scale,
        "tm",
        scatter_dimension=0,
        tiled=True,
    )


def solution(mesh):
    return jax.shard_map(
        on_device,
        mesh=mesh,
        in_specs=(
            P(("groups", "chan", "sub"), "tm"),
            P(("groups", "chan", "sub"), None),
            P("groups"),
        ),
        out_specs=P("tm", None, ("groups", "chan", "sub")),
        check_vma=False,
    )
```

profile of v0, /device:TPU:0, one launch (start us, length us, event | category | flops | bytes accessed | tf_op | source)
XLA Modules:
  0.0 404.3 jit_solution(17135391241325937660)
XLA Ops:
  6.5 1.0 fusion.81
  7.5 1.3 collective-permute-start.1
  8.8 4.9 %collective-permute-start = (f32[128,96]{1,0:T(8,128)S(1)}, f32[128,96]{1,0:T(8,128)S(1)}, u32[]{:S(2)}, u32[]{:S(2)}) collective-permute-start(f32[128,96]{1,0:T(8,128)S(1)} %get-tuple-element.115), channel_id=1, source_target_pairs={{0,2},{1,3},{4,6},{5,7},{8,10},{9,11},{12,14},{13,15},{16,18},{17,... | collective-permute-start | bytes 147464 | tf_op jit(solution)/shard_map/ppermute | solution.py:15
  13.7 0.9 slice_bitcast_fusion.61
  14.6 1.0 slice_bitcast_fusion.63
  15.6 1.0 slice_bitcast_fusion.64
  16.6 1.0 slice_bitcast_fusion.62
  17.6 0.7 and_select_fusion
  18.3 0.7 broadcast_compare_fusion
  18.9 0.2 convert_reduce_fusion
  19.1 0.0 collective-permute-done.1
  19.1 0.0 collective-permute-done
  19.1 2.9 concatenate.3
  22.1 42.9 %fusion.2 = bf16[128,4224]{1,0:T(8,128)(2,1)} fusion(f32[128,4288]{1,0:T(8,128)S(1)} %concatenate.3, f32[128]{0:T(128)S(1)} %get-tuple-element.179, f32[128]{0:T(128)S(1)} %get-tuple-element.180, f32[128]{0:T(128)S(1)} %get-tuple-element.117, f32[128]{0:T(128)S(1)} %get-tuple-element.118, f32[128]{0:T(128)S(1)} %get-tuple-element.119, ...), kind=kLoop, calls=%fused_computation.9 | loop fusion | flops 70828032 | bytes 141693568 | tf_op jit(solution)/shard_map/convert_element_type | solution.py:68
  65.0 2.4 convolution_convert_fusion.1
  67.4 0.0 all-gather.2.cloned.1.call-update
  67.4 0.2 reduce-scatter.2.cloned.1.call-start
  67.7 23.6 %all-gather.2.cloned.1.call-done = bf16[128,4096]{1,0:T(8,128)(2,1)} async-done(((bf16[16,4096]{1,0:T(8,128)(2,1)}), bf16[128,4096]{1,0:T(8,128)(2,1)}) %all-gather.2.cloned.1.call-update) | async-done | bytes 1048592 | tf_op jit(solution)/shard_map/all_gather | solution.py:87
  91.3 2.8 convolution_convert_fusion
  94.0 186.1 %while.14 = (s32[]{:T(128)}, f32[128,128,129]{1,0,2:T(8,128)}, bf16[128,4224]{1,0:T(8,128)(2,1)}, bf16[128,4096]{1,0:T(8,128)(2,1)}, s32[]{:T(128)}, /*index=5*/s32[]{:T(128)}, s32[]{:T(128)}, s32[]{:T(128)}, s32[]{:T(128)}) while((s32[]{:T(128)}, f32[128,128,129]{1,0,2:T(8,128)}, bf16[128,4224]{1,0:T(8,128)(2,1)}, ...), condition=%wide.region_2.3_spmd.clone, body=%wide.region_1.2_spmd.clone.sunk | while | flops 2168487936 | bytes 18383036 | solution.py:50
  94.0 0.9 dynamic-slice_bitcast_fusion.5
  95.0 0.2 copy.18
  95.1 0.9 dynamic-slice_bitcast_fusion.4
  96.1 0.2 copy.17
  96.3 19.1 %select_add_fusion.2 = f32[128,128,129]{1,0,2:T(8,128)} fusion(f32[128,128,129]{1,0,2:T(8,128)} %get-tuple-element.216, pred[]{:T(512)S(6)} %compare.6, bf16[128,1,640]{0,1,2:T(2,128)(2,1)S(1)} %copy.17, bf16[128,1,512]{0,1,2:T(2,128)(2,1)S(1)} %copy.18), kind=kOutput, calls=%fused_computation.clone.1 | convolution fusion | flops 2168487936 | bytes 17203200 | tf_op jit(solution)/shard_map/while/body/eval_jaxpr/conv_general_dilated | solution.py:39
  115.4 0.9 dynamic-slice_bitcast_fusion.5
  116.3 0.2 copy.18
  116.5 0.9 dynamic-slice_bitcast_fusion.4
  117.4 0.2 copy.17
  117.6 21.3 %select_add_fusion.2 = f32[128,128,129]{1,0,2:T(8,128)} fusion(f32[128,128,129]{1,0,2:T(8,128)} %get-tuple-element.216, pred[]{:T(512)S(6)} %compare.6, bf16[128,1,640]{0,1,2:T(2,128)(2,1)S(1)} %copy.17, bf16[128,1,512]{0,1,2:T(2,128)(2,1)S(1)} %copy.18), kind=kOutput, calls=%fused_computation.clone.1 | convolution fusion | flops 2168487936 | bytes 17203200 | tf_op jit(solution)/shard_map/while/body/eval_jaxpr/conv_general_dilated | solution.py:39
  138.9 0.9 dynamic-slice_bitcast_fusion.5
  139.9 0.2 copy.18
  140.0 0.9 dynamic-slice_bitcast_fusion.4
  141.0 0.2 copy.17
  141.2 21.3 %select_add_fusion.2 = f32[128,128,129]{1,0,2:T(8,128)} fusion(f32[128,128,129]{1,0,2:T(8,128)} %get-tuple-element.216, pred[]{:T(512)S(6)} %compare.6, bf16[128,1,640]{0,1,2:T(2,128)(2,1)S(1)} %copy.17, bf16[128,1,512]{0,1,2:T(2,128)(2,1)S(1)} %copy.18), kind=kOutput, calls=%fused_computation.clone.1 | convolution fusion | flops 2168487936 | bytes 17203200 | tf_op jit(solution)/shard_map/while/body/eval_jaxpr/conv_general_dilated | solution.py:39
  162.5 0.9 dynamic-slice_bitcast_fusion.5
  163.4 0.2 copy.18
  163.6 0.9 dynamic-slice_bitcast_fusion.4
  164.5 0.2 copy.17
  164.7 21.3 %select_add_fusion.2 = f32[128,128,129]{1,0,2:T(8,128)} fusion(f32[128,128,129]{1,0,2:T(8,128)} %get-tuple-element.216, pred[]{:T(512)S(6)} %compare.6, bf16[128,1,640]{0,1,2:T(2,128)(2,1)S(1)} %copy.17, bf16[128,1,512]{0,1,2:T(2,128)(2,1)S(1)} %copy.18), kind=kOutput, calls=%fused_computation.clone.1 | convolution fusion | flops 2168487936 | bytes 17203200 | tf_op jit(solution)/shard_map/while/body/eval_jaxpr/conv_general_dilated | solution.py:39
  186.0 0.9 dynamic-slice_bitcast_fusion.5
  186.9 0.2 copy.18
  187.1 0.9 dynamic-slice_bitcast_fusion.4
  188.0 0.2 copy.17
  188.3 21.3 %select_add_fusion.2 = f32[128,128,129]{1,0,2:T(8,128)} fusion(f32[128,128,129]{1,0,2:T(8,128)} %get-tuple-element.216, pred[]{:T(512)S(6)} %compare.6, bf16[128,1,640]{0,1,2:T(2,128)(2,1)S(1)} %copy.17, bf16[128,1,512]{0,1,2:T(2,128)(2,1)S(1)} %copy.18), kind=kOutput, calls=%fused_computation.clone.1 | convolution fusion | flops 2168487936 | bytes 17203200 | tf_op jit(solution)/shard_map/while/body/eval_jaxpr/conv_general_dilated | solution.py:39
  209.6 0.9 dynamic-slice_bitcast_fusion.5
  210.5 0.2 copy.18
  210.6 0.9 dynamic-slice_bitcast_fusion.4
  211.6 0.2 copy.17
  211.8 21.3 %select_add_fusion.2 = f32[128,128,129]{1,0,2:T(8,128)} fusion(f32[128,128,129]{1,0,2:T(8,128)} %get-tuple-element.216, pred[]{:T(512)S(6)} %compare.6, bf16[128,1,640]{0,1,2:T(2,128)(2,1)S(1)} %copy.17, bf16[128,1,512]{0,1,2:T(2,128)(2,1)S(1)} %copy.18), kind=kOutput, calls=%fused_computation.clone.1 | convolution fusion | flops 2168487936 | bytes 17203200 | tf_op jit(solution)/shard_map/while/body/eval_jaxpr/conv_general_dilated | solution.py:39
  233.1 0.9 dynamic-slice_bitcast_fusion.5
  234.0 0.2 copy.18
  234.2 0.9 dynamic-slice_bitcast_fusion.4
  235.1 0.2 copy.17
  235.3 21.3 %select_add_fusion.2 = f32[128,128,129]{1,0,2:T(8,128)} fusion(f32[128,128,129]{1,0,2:T(8,128)} %get-tuple-element.216, pred[]{:T(512)S(6)} %compare.6, bf16[128,1,640]{0,1,2:T(2,128)(2,1)S(1)} %copy.17, bf16[128,1,512]{0,1,2:T(2,128)(2,1)S(1)} %copy.18), kind=kOutput, calls=%fused_computation.clone.1 | convolution fusion | flops 2168487936 | bytes 17203200 | tf_op jit(solution)/shard_map/while/body/eval_jaxpr/conv_general_dilated | solution.py:39
  256.6 0.9 dynamic-slice_bitcast_fusion.5
  257.5 0.2 copy.18
  257.7 0.9 dynamic-slice_bitcast_fusion.4
  258.7 0.2 copy.17
  258.9 21.3 %select_add_fusion.2 = f32[128,128,129]{1,0,2:T(8,128)} fusion(f32[128,128,129]{1,0,2:T(8,128)} %get-tuple-element.216, pred[]{:T(512)S(6)} %compare.6, bf16[128,1,640]{0,1,2:T(2,128)(2,1)S(1)} %copy.17, bf16[128,1,512]{0,1,2:T(2,128)(2,1)S(1)} %copy.18), kind=kOutput, calls=%fused_computation.clone.1 | convolution fusion | flops 2168487936 | bytes 17203200 | tf_op jit(solution)/shard_map/while/body/eval_jaxpr/conv_general_dilated | solution.py:39
  280.2 9.0 %copy.14 = f32[128,128,129]{0,1,2:T(8,128)} copy(f32[128,128,129]{1,0,2:T(8,128)} %get-tuple-element.84) | data formatting | bytes 16908288 | tf_op jit(solution)/shard_map/while | solution.py:50
  289.2 8.5 %multiply_bitcast_fusion = f32[128,129,128]{2,0,1:T(8,128)} fusion(f32[128,128,129]{0,1,2:T(8,128)} %copy.14), kind=kLoop, calls=%fused_computation.3 | loop fusion | flops 2113536 | bytes 16908288 | tf_op jit(solution)/shard_map/mul | solution.py:96
  297.7 0.0 reduce-scatter.2.cloned.1.call-update
  297.7 99.8 %reduce-scatter.2.cloned.1.call-done = f32[64,129,128]{2,0,1:T(8,128)} async-done(((f32[128,129,128]{2,0,1:T(8,128)}), f32[64,129,128]{2,0,1:T(8,128)}) %reduce-scatter.2.cloned.1.call-update) | async-done | bytes 4227088 | tf_op jit(solution)/shard_map/reduce_scatter | solution.py:95
  (4 shorter events, 0.0 us)
Async XLA Ops:
  6.5 84.7 %all-gather.2.cloned.1.call-start = ((), (), s32[]{:S(2)}) async-start(), calls=%async_computation.1 | async-start | bytes 1179648 | tf_op jit(solution)/shard_map/all_gather | solution.py:87
  7.5 11.6 %collective-permute-start.1 = (f32[128,96]{1,0:T(8,128)S(1)}, f32[128,96]{1,0:T(8,128)S(1)}, u32[]{:S(2)}, u32[]{:S(2)}) collective-permute-start(f32[128,96]{1,0:T(8,128)S(1)} %get-tuple-element.114), channel_id=1, source_target_pairs={{2,0},{3,1},{6,4},{7,5},{10,8},{11,9},{14,12},{15,13},{18,16},{19,... | collective-permute-start | bytes 147464 | tf_op jit(solution)/shard_map/ppermute | solution.py:18
  8.8 10.3 %collective-permute-start = (f32[128,96]{1,0:T(8,128)S(1)}, f32[128,96]{1,0:T(8,128)S(1)}, u32[]{:S(2)}, u32[]{:S(2)}) collective-permute-start(f32[128,96]{1,0:T(8,128)S(1)} %get-tuple-element.115), channel_id=1, source_target_pairs={{0,2},{1,3},{4,6},{5,7},{8,10},{9,11},{12,14},{13,15},{16,18},{17,... | collective-permute-start | bytes 147464 | tf_op jit(solution)/shard_map/ppermute | solution.py:15
  67.4 330.1 %reduce-scatter.2.cloned.1.call-start = ((), (), s32[]{:S(2)}) async-start(), calls=%async_computation.2 | async-start | bytes 12681216 | tf_op jit(solution)/shard_map/reduce_scatter | solution.py:95
Sparse Core Ops, SparseCore 0:
  67.5 23.6 all-gather.1
  297.8 99.6 reduce-scatter.1
where the time goes:
time: 405 us; the launch traced here: 404 us
  matrix products  173 us (43%)
  waiting for transfers between devices  123 us (30%)
  other arithmetic  52.9 us (13%)
  local copies, waits for them, and re-layouts  34.5 us (9%)
  between operations  13.5 us (3%)
  starting transfers between devices  6.39 us (2%)
    conv_general_dilated x8, matrix products, advance(): lax.conv_general_dilated(window[:, None, :], rows_here[:, None, :], (1,),...  168 us
    reduce_scatter x1, waiting for transfers between devices, on_device(): lax.psum_scatter(jnp.transpose(summed[:, :, ::-1], (1, 2, 0)) * norm_scal...  99.8 us
    convert_element_type x1, other arithmetic, on_device(): padded = jnp.where(inside[None, :], whitened_ext, 0.0).astype(jnp.bfloat16)  42.9 us
    all_gather x1, waiting for transfers between devices, on_device(): segment = lax.all_gather(slot_rows, ('chan', 'sub'), axis=0, tiled=True)  23.6 us
    broadcast_in_dim x16, local copies, waits for them, and re-layouts, advance(): window[:, None, :]  9.16 us
    while x1, local copies, waits for them, and re-layouts, correlate(): return lax.fori_loop(0, block_count, advance, start_sum)  9 us
    broadcast_in_dim x16, local copies, waits for them, and re-layouts, advance(): rows_here[:, None, :]  8.59 us
    mul x1, other arithmetic, on_device(): jnp.transpose(summed[:, :, ::-1], (1, 2, 0)) * norm_scale  8.51 us
  transfers between devices with their start and end apart: 4, of which 2 were waited for; matrix products, arithmetic and copies ran while one was open for 1% of the time, Pallas kernels for 0%

commit v1 on v0

--- a/solution.py
+++ b/solution.py
@@ -5,6 +5,27 @@
 from jax.sharding import PartitionSpec as P
 
 LAGS = 129
+
+
+def in_order(blocks, dim):
+    blocks = jnp.moveaxis(blocks, 0, dim)
+    lengths = blocks.shape
+    return blocks.reshape(*lengths[:dim], lengths[dim] * lengths[dim + 1], *lengths[dim + 2 :])
+
+
+def grow_blocks(x, axis):
+    length, index = (lax.axis_size(axis), lax.axis_index(axis))
+    pieces, bit = (x[None], 1)
+    while bit < length:
+        theirs = lax.ppermute(pieces, axis, [(i, i ^ bit) for i in range(length)])
+        low = index & bit == 0
+        pieces = jnp.concatenate([jnp.where(low, pieces, theirs), jnp.where(low, theirs, pieces)])
+        bit *= 2
+    return pieces
+
+
+def gather_by_bits(x, axis, dim):
+    return in_order(grow_blocks(x, axis), dim)
 
 
 def padded_2(block, sides, width):
@@ -84,7 +105,7 @@
     picker = jnp.dot(choose, onehot, preferred_element_type=jnp.float32).astype(jnp.bfloat16)
     slot_rows = jnp.dot(picker, whitened, preferred_element_type=jnp.float32).astype(jnp.bfloat16)
     slot_id = owners * slot_most + rank_in
-    segment = lax.all_gather(slot_rows, ("chan", "sub"), axis=0, tiled=True)
+    segment = gather_by_bits(slot_rows, ("chan", "sub"), 0)
     row_count = segment.shape[0]
     select = (slot_id[:, None] == jnp.arange(row_count, dtype=jnp.int32)[None, :]).astype(
         jnp.bfloat16

time: 405 us -> 417 us (1.030)
  waiting for transfers between devices: 123 us -> 131 us
  starting transfers between devices: 6.39 us -> 11.8 us
    ppermute x0 -> x3, waiting for transfers between devices: none -> 30.7 us  [grow_blocks(): theirs = lax.ppermute(pieces, axis, [(i, i ^ bit) for i in range(length)])]
    all_gather x1 -> x0, waiting for transfers between devices: 23.6 us -> none  [on_device(): segment = lax.all_gather(slot_rows, ('chan', 'sub'), axis=0, tiled=True)]
    ppermute x0 -> x3, starting transfers between devices: none -> 5.65 us  [grow_blocks(): theirs = lax.ppermute(pieces, axis, [(i, i ^ bit) for i in range(length)])]
  transfers between devices with their start and end apart: 4 -> 6, of which waited for: 2 -> 4; matrix products, arithmetic and copies ran while one was open for 1% -> 1% of each run, Pallas kernels for 0% -> 0%
where the time goes in v1:
time: 417 us; the launch traced here: 416 us
  matrix products  172 us (41%)
  waiting for transfers between devices  131 us (31%)
  other arithmetic  53.2 us (13%)
  local copies, waits for them, and re-layouts  34.5 us (8%)
  between operations  13.5 us (3%)
  starting transfers between devices  11.8 us (3%)
    conv_general_dilated x8, matrix products, advance(): lax.conv_general_dilated(window[:, None, :], rows_here[:, None, :], (1,),...  168 us
    reduce_scatter x1, waiting for transfers between devices, on_device(): lax.psum_scatter(jnp.transpose(summed[:, :, ::-1], (1, 2, 0)) * norm_scal...  100 us
    convert_element_type x1, other arithmetic, on_device(): padded = jnp.where(inside[None, :], whitened_ext, 0.0).astype(jnp.bfloat16)  42.9 us
    ppermute x3, waiting for transfers between devices, grow_blocks(): theirs = lax.ppermute(pieces, axis, [(i, i ^ bit) for i in range(length)])  30.7 us
    broadcast_in_dim x16, local copies, waits for them, and re-layouts, advance(): window[:, None, :]  9.16 us
    while x1, local copies, waits for them, and re-layouts, correlate(): return lax.fori_loop(0, block_count, advance, start_sum)  8.99 us
    broadcast_in_dim x16, local copies, waits for them, and re-layouts, advance(): rows_here[:, None, :]  8.59 us
    mul x1, other arithmetic, on_device(): jnp.transpose(summed[:, :, ::-1], (1, 2, 0)) * norm_scale  8.52 us
  transfers between devices with their start and end apart: 6, of which 4 were waited for; matrix products, arithmetic and copies ran while one was open for 1% of the time, Pallas kernels for 0%

profile of v1, /device:TPU:0, one launch (start us, length us, event | category | flops | bytes accessed | tf_op | source)
XLA Modules:
  0.0 415.8 jit_solution(26174954267684269)
XLA Ops:
  6.5 1.0 fusion.82
  7.5 1.3 collective-permute-start.1
  8.8 4.9 %collective-permute-start = (f32[128,96]{1,0:T(8,128)S(1)}, f32[128,96]{1,0:T(8,128)S(1)}, u32[]{:S(2)}, u32[]{:S(2)}) collective-permute-start(f32[128,96]{1,0:T(8,128)S(1)} %get-tuple-element.115), channel_id=1, source_target_pairs={{0,2},{1,3},{4,6},{5,7},{8,10},{9,11},{12,14},{13,15},{16,18},{17,... | collective-permute-start | bytes 147464 | tf_op jit(solution)/shard_map/ppermute | solution.py:36
  13.7 0.9 slice_bitcast_fusion.61
  14.6 1.0 slice_bitcast_fusion.63
  15.6 1.0 slice_bitcast_fusion.64
  16.6 1.0 slice_bitcast_fusion.62
  17.6 0.7 and_select_fusion
  18.3 0.7 broadcast_compare_fusion
  18.9 0.2 convert_reduce_fusion
  19.1 2.9 concatenate.12
  22.1 42.9 %fusion.3 = bf16[128,4224]{1,0:T(8,128)(2,1)} fusion(f32[128,4288]{1,0:T(8,128)S(1)} %concatenate.12, f32[128]{0:T(128)S(1)} %get-tuple-element.185, f32[128]{0:T(128)S(1)} %get-tuple-element.186, f32[128]{0:T(128)S(1)} %get-tuple-element.123, f32[128]{0:T(128)S(1)} %get-tuple-element.124, f32[128]{0:T(128)S(1)} %get-tuple-element.125, ...), kind=kLoop, calls=%fused_computation.10 | loop fusion | flops 70828032 | bytes 141693568 | tf_op jit(solution)/shard_map/convert_element_type | solution.py:89
  65.0 1.7 fusion
  66.8 1.3 collective-permute-done.2
  68.2 2.8 collective-permute-start.3
  70.9 6.6 %collective-permute-done.3 = bf16[2,16,4096]{2,1,0:T(8,128)(2,1)S(1)} collective-permute-done((bf16[2,16,4096]{2,1,0:T(8,128)(2,1)S(1)}, bf16[2,16,4096]{2,1,0:T(8,128)(2,1)S(1)}, u32[]{:S(2)}, u32[]{:S(2)}) %collective-permute-start.3) | collective-permute-done | bytes 262176 | tf_op jit(solution)/shard_map/ppermute | solution.py:20
  77.7 2.8 collective-permute-start.4
  80.5 22.8 %collective-permute-done.4 = bf16[4,16,4096]{2,1,0:T(8,128)(2,1)S(1)} collective-permute-done((bf16[4,16,4096]{2,1,0:T(8,128)(2,1)S(1)}, bf16[4,16,4096]{2,1,0:T(8,128)(2,1)S(1)}, u32[]{:S(2)}, u32[]{:S(2)}) %collective-permute-start.4) | collective-permute-done | bytes 524320 | tf_op jit(solution)/shard_map/ppermute | solution.py:20
  103.3 0.1 pad_maximum_fusion
  103.4 1.5 convolution_convert_fusion
  105.0 186.2 %while.14 = (s32[]{:T(128)}, f32[128,128,129]{1,0,2:T(8,128)}, bf16[128,4224]{1,0:T(8,128)(2,1)}, bf16[128,4096]{1,0:T(8,128)(2,1)}, s32[]{:T(128)}, /*index=5*/s32[]{:T(128)}, s32[]{:T(128)}, s32[]{:T(128)}, s32[]{:T(128)}) while((s32[]{:T(128)}, f32[128,128,129]{1,0,2:T(8,128)}, bf16[128,4224]{1,0:T(8,128)(2,1)}, ...), condition=%wide.region_2.3_spmd.clone, body=%wide.region_1.2_spmd.clone.sunk | while | flops 2168487936 | bytes 18383036 | solution.py:71
  105.0 0.9 dynamic-slice_bitcast_fusion.5
  105.9 0.2 copy.18
  106.1 0.9 dynamic-slice_bitcast_fusion.4
  107.0 0.2 copy.17
  107.2 19.1 %select_add_fusion.2 = f32[128,128,129]{1,0,2:T(8,128)} fusion(f32[128,128,129]{1,0,2:T(8,128)} %get-tuple-element.222, pred[]{:T(512)S(6)} %compare.6, bf16[128,1,640]{0,1,2:T(2,128)(2,1)S(1)} %copy.17, bf16[128,1,512]{0,1,2:T(2,128)(2,1)S(1)} %copy.18), kind=kOutput, calls=%fused_computation.clone.1 | convolution fusion | flops 2168487936 | bytes 17203200 | tf_op jit(solution)/shard_map/while/body/eval_jaxpr/conv_general_dilated | solution.py:60
  126.4 0.9 dynamic-slice_bitcast_fusion.5
  127.3 0.2 copy.18
  127.4 0.9 dynamic-slice_bitcast_fusion.4
  128.4 0.2 copy.17
  128.6 21.3 %select_add_fusion.2 = f32[128,128,129]{1,0,2:T(8,128)} fusion(f32[128,128,129]{1,0,2:T(8,128)} %get-tuple-element.222, pred[]{:T(512)S(6)} %compare.6, bf16[128,1,640]{0,1,2:T(2,128)(2,1)S(1)} %copy.17, bf16[128,1,512]{0,1,2:T(2,128)(2,1)S(1)} %copy.18), kind=kOutput, calls=%fused_computation.clone.1 | convolution fusion | flops 2168487936 | bytes 17203200 | tf_op jit(solution)/shard_map/while/body/eval_jaxpr/conv_general_dilated | solution.py:60
  149.9 0.9 dynamic-slice_bitcast_fusion.5
  150.8 0.2 copy.18
  151.0 0.9 dynamic-slice_bitcast_fusion.4
  151.9 0.2 copy.17
  152.1 21.3 %select_add_fusion.2 = f32[128,128,129]{1,0,2:T(8,128)} fusion(f32[128,128,129]{1,0,2:T(8,128)} %get-tuple-element.222, pred[]{:T(512)S(6)} %compare.6, bf16[128,1,640]{0,1,2:T(2,128)(2,1)S(1)} %copy.17, bf16[128,1,512]{0,1,2:T(2,128)(2,1)S(1)} %copy.18), kind=kOutput, calls=%fused_computation.clone.1 | convolution fusion | flops 2168487936 | bytes 17203200 | tf_op jit(solution)/shard_map/while/body/eval_jaxpr/conv_general_dilated | solution.py:60
  173.4 0.9 dynamic-slice_bitcast_fusion.5
  174.4 0.2 copy.18
  174.5 0.9 dynamic-slice_bitcast_fusion.4
  175.5 0.2 copy.17
  175.7 21.3 %select_add_fusion.2 = f32[128,128,129]{1,0,2:T(8,128)} fusion(f32[128,128,129]{1,0,2:T(8,128)} %get-tuple-element.222, pred[]{:T(512)S(6)} %compare.6, bf16[128,1,640]{0,1,2:T(2,128)(2,1)S(1)} %copy.17, bf16[128,1,512]{0,1,2:T(2,128)(2,1)S(1)} %copy.18), kind=kOutput, calls=%fused_computation.clone.1 | convolution fusion | flops 2168487936 | bytes 17203200 | tf_op jit(solution)/shard_map/while/body/eval_jaxpr/conv_general_dilated | solution.py:60
  197.0 0.9 dynamic-slice_bitcast_fusion.5
  197.9 0.2 copy.18
  198.1 0.9 dynamic-slice_bitcast_fusion.4
  199.0 0.2 copy.17
  199.2 21.3 %select_add_fusion.2 = f32[128,128,129]{1,0,2:T(8,128)} fusion(f32[128,128,129]{1,0,2:T(8,128)} %get-tuple-element.222, pred[]{:T(512)S(6)} %compare.6, bf16[128,1,640]{0,1,2:T(2,128)(2,1)S(1)} %copy.17, bf16[128,1,512]{0,1,2:T(2,128)(2,1)S(1)} %copy.18), kind=kOutput, calls=%fused_computation.clone.1 | convolution fusion | flops 2168487936 | bytes 17203200 | tf_op jit(solution)/shard_map/while/body/eval_jaxpr/conv_general_dilated | solution.py:60
  220.5 0.9 dynamic-slice_bitcast_fusion.5
  221.4 0.2 copy.18
  221.6 0.9 dynamic-slice_bitcast_fusion.4
  222.6 0.2 copy.17
  222.8 21.3 %select_add_fusion.2 = f32[128,128,129]{1,0,2:T(8,128)} fusion(f32[128,128,129]{1,0,2:T(8,128)} %get-tuple-element.222, pred[]{:T(512)S(6)} %compare.6, bf16[128,1,640]{0,1,2:T(2,128)(2,1)S(1)} %copy.17, bf16[128,1,512]{0,1,2:T(2,128)(2,1)S(1)} %copy.18), kind=kOutput, calls=%fused_computation.clone.1 | convolution fusion | flops 2168487936 | bytes 17203200 | tf_op jit(solution)/shard_map/while/body/eval_jaxpr/conv_general_dilated | solution.py:60
  244.1 0.9 dynamic-slice_bitcast_fusion.5
  245.0 0.2 copy.18
  245.2 0.9 dynamic-slice_bitcast_fusion.4
  246.1 0.2 copy.17
  246.3 21.3 %select_add_fusion.2 = f32[128,128,129]{1,0,2:T(8,128)} fusion(f32[128,128,129]{1,0,2:T(8,128)} %get-tuple-element.222, pred[]{:T(512)S(6)} %compare.6, bf16[128,1,640]{0,1,2:T(2,128)(2,1)S(1)} %copy.17, bf16[128,1,512]{0,1,2:T(2,128)(2,1)S(1)} %copy.18), kind=kOutput, calls=%fused_computation.clone.1 | convolution fusion | flops 2168487936 | bytes 17203200 | tf_op jit(solution)/shard_map/while/body/eval_jaxpr/conv_general_dilated | solution.py:60
  267.6 0.9 dynamic-slice_bitcast_fusion.5
  268.5 0.2 copy.18
  268.7 0.9 dynamic-slice_bitcast_fusion.4
  269.6 0.2 copy.17
  269.9 21.3 %select_add_fusion.2 = f32[128,128,129]{1,0,2:T(8,128)} fusion(f32[128,128,129]{1,0,2:T(8,128)} %get-tuple-element.222, pred[]{:T(512)S(6)} %compare.6, bf16[128,1,640]{0,1,2:T(2,128)(2,1)S(1)} %copy.17, bf16[128,1,512]{0,1,2:T(2,128)(2,1)S(1)} %copy.18), kind=kOutput, calls=%fused_computation.clone.1 | convolution fusion | flops 2168487936 | bytes 17203200 | tf_op jit(solution)/shard_map/while/body/eval_jaxpr/conv_general_dilated | solution.py:60
  291.2 9.0 %copy.14 = f32[128,128,129]{0,1,2:T(8,128)} copy(f32[128,128,129]{1,0,2:T(8,128)} %get-tuple-element.84) | data formatting | bytes 16908288 | tf_op jit(solution)/shard_map/while | solution.py:71
  300.1 8.5 %multiply_bitcast_fusion = f32[128,129,128]{2,0,1:T(8,128)} fusion(f32[128,128,129]{0,1,2:T(8,128)} %copy.14), kind=kLoop, calls=%fused_computation.3 | loop fusion | flops 2113536 | bytes 16908288 | tf_op jit(solution)/shard_map/mul | solution.py:117
  308.7 100.3 %reduce-scatter.2.cloned.1.call-done = f32[64,129,128]{2,0,1:T(8,128)} async-done(((f32[128,129,128]{2,0,1:T(8,128)}), f32[64,129,128]{2,0,1:T(8,128)}) %reduce-scatter.2.cloned.1.call-update) | async-done | bytes 4227088 | tf_op jit(solution)/shard_map/reduce_scatter | solution.py:116
  (13 shorter events, 0.3 us)
Async XLA Ops:
  6.5 402.4 %reduce-scatter.2.cloned.1.call-start = ((), (), s32[]{:S(2)}) async-start(), calls=%async_computation.1 | async-start | bytes 12681216 | tf_op jit(solution)/shard_map/reduce_scatter | solution.py:116
  7.5 11.6 %collective-permute-start.1 = (f32[128,96]{1,0:T(8,128)S(1)}, f32[128,96]{1,0:T(8,128)S(1)}, u32[]{:S(2)}, u32[]{:S(2)}) collective-permute-start(f32[128,96]{1,0:T(8,128)S(1)} %get-tuple-element.114), channel_id=1, source_target_pairs={{2,0},{3,1},{6,4},{7,5},{10,8},{11,9},{14,12},{15,13},{18,16},{19,... | collective-permute-start | bytes 147464 | tf_op jit(solution)/shard_map/ppermute | solution.py:39
  8.8 10.3 %collective-permute-start = (f32[128,96]{1,0:T(8,128)S(1)}, f32[128,96]{1,0:T(8,128)S(1)}, u32[]{:S(2)}, u32[]{:S(2)}) collective-permute-start(f32[128,96]{1,0:T(8,128)S(1)} %get-tuple-element.115), channel_id=1, source_target_pairs={{0,2},{1,3},{4,6},{5,7},{8,10},{9,11},{12,14},{13,15},{16,18},{17,... | collective-permute-start | bytes 147464 | tf_op jit(solution)/shard_map/ppermute | solution.py:36
  66.7 1.4 collective-permute-start.2
  68.2 9.4 %collective-permute-start.3 = (bf16[2,16,4096]{2,1,0:T(8,128)(2,1)S(1)}, bf16[2,16,4096]{2,1,0:T(8,128)(2,1)S(1)}, u32[]{:S(2)}, u32[]{:S(2)}) collective-permute-start(bf16[2,16,4096]{2,1,0:T(8,128)(2,1)S(1)} %pad_maximum_fusion.2), channel_id=1, source_target_pairs={{0,4},{1,5},{4,0},{5,1},{8,12},{9,13},{12,8},{13,9},{2,6},{3,7},{6... | collective-permute-start | bytes 786440 | tf_op jit(solution)/shard_map/ppermute | solution.py:20
  77.7 25.6 %collective-permute-start.4 = (bf16[4,16,4096]{2,1,0:T(8,128)(2,1)S(1)}, bf16[4,16,4096]{2,1,0:T(8,128)(2,1)S(1)}, u32[]{:S(2)}, u32[]{:S(2)}) collective-permute-start(bf16[4,16,4096]{2,1,0:T(8,128)(2,1)S(1)} %pad_maximum_fusion.1), channel_id=1, source_target_pairs={{0,8},{1,9},{4,12},{5,13},{8,0},{9,1},{12,4},{13,5},{2,10},{3,11},... | collective-permute-start | bytes 1572872 | tf_op jit(solution)/shard_map/ppermute | solution.py:20
Sparse Core Ops, SparseCore 0:
  308.8 100.1 reduce-scatter.1
